TPU v7x, 32 devices: a whole 2x2x4 slice. The times are simulated.
32 devices in a mesh: sample: 2 (over y), harm: 16 (over z, x, core).
Axes of the slice: x: 2, y: 2, z: 4, core: 2. Of those that a mesh axis runs over, the one named last changes fastest.
Arguments:
- inputs: bfloat16 [128, 64, 512], P('sample', 'harm'), parts along dimension 0, may hold values from -6 to 6
- col_list: int32 [128], P('sample'), parts along dimension 0, may hold values from 0 to 63, each once
- row_list: int32 [128], P('sample'), parts along dimension 0, may hold values from 0 to 63, each once
- gain_attn: float32 [512], replicated, may hold values from 0.25 to 1.75
- w_qkv: bfloat16 [512, 1536], replicated
- w_out: bfloat16 [512, 512], replicated, may hold values from -0.25 to 0.25
- gain_ffn: float32 [512], replicated, may hold values from 0.25 to 1.75
- w_gate: bfloat16 [512, 1024], P('harm'), may hold values from -0.25 to 0.25
- w_up: bfloat16 [512, 1024], P('harm'), may hold values from -0.25 to 0.25
- w_down: bfloat16 [1024, 512], P('harm'), may hold values from -0.1875 to 0.1875
Outputs:
- result: bfloat16 [64, 128, 512], P('harm', 'sample'), parts along dimension 1
There are 2 independent parts, one for each index of `sample`. A program takes and returns all parts, laid end to end along the dimension named above; an argument that names none is the same for every part. Nothing has to cross between parts.
Inputs may be any that keep to these rules, and one draw needn't show every extreme that they name: col_list names every order m of 0 to 63 exactly once. row_list names every degree ell of 0 to 63 exactly once.
All inputs are finite; a program needn't handle non-finite values.
Results may differ from a plain program's by a relative error of at most 0.0073.
Values may be sent and summed in bfloat16 or wider, within the bound.
A program may use at most 64 MiB of HBM per device.

v0:
```python
import jax
import jax.numpy as jnp
from jax import lax
from jax.sharding import PartitionSpec as P

HEADS = 8
WIN = 256
eps = 1e-06
masked = -1e30


def rms_scale(values, gain):
    values = values.astype(jnp.float32)
    mean_sq = jnp.mean(values * values, axis=-1, keepdims=True)
    return values * lax.rsqrt(mean_sq + eps) * gain


def split_heads(block, start, split, head_dim):
    piece = block[..., start : start + split]
    return piece.reshape(piece.shape[:-1] + (split // head_dim, head_dim))


def softmax_rounded(scores):
    top = jnp.max(scores, axis=-1, keepdims=True)
    weights = jnp.exp(scores - top)
    return (weights / jnp.sum(weights, axis=-1, keepdims=True)).astype(jnp.bfloat16)


def column_attention(query, keys, values, starts, scale):
    length = query.shape[0]
    here = jnp.arange(length, dtype=jnp.int32)
    offset = here[None, :] - here[:, None]
    band = (offset >= -(WIN // 2)) & (offset < WIN // 2)
    allowed = band[None] & (here[None, None, :] >= starts[:, None, None])
    scores = jnp.einsum("lchd,kchd->chlk", query, keys, preferred_element_type=jnp.float32) * scale
    scores = jnp.where(allowed[:, None], scores, masked)
    probs = softmax_rounded(scores)
    mixed = jnp.einsum("chlk,kchd->lchd", probs, values, preferred_element_type=jnp.float32)
    return mixed.astype(jnp.bfloat16)


def row_attention(query, keys, values, marks, limits, scale):
    diff = marks[None, :] - marks[:, None]
    band = (diff >= -(WIN // 2)) & (diff < WIN // 2)
    allowed = band[None] & (marks[None, None, :] <= limits[:, None, None])
    scores = jnp.einsum("ishd,ithd->ihst", query, keys, preferred_element_type=jnp.float32) * scale
    scores = jnp.where(allowed[:, None], scores, masked)
    probs = softmax_rounded(scores)
    mixed = jnp.einsum("ihst,ithd->ishd", probs, values, preferred_element_type=jnp.float32)
    return mixed.astype(jnp.bfloat16)


def per_device(inputs, col_list, row_list, gain_attn, w_qkv, w_out, gain_ffn, w_gate, w_up, w_down):
    place = lax.axis_index("harm")
    groups = lax.axis_size("harm")
    length, cols, width = inputs.shape
    rows_here = length // groups
    head_dim = width // HEADS
    half = HEADS // 2
    split = half * head_dim
    scale = head_dim ** (-0.5)
    my_cols = lax.dynamic_slice_in_dim(col_list, place * cols, cols)
    my_rows = lax.dynamic_slice_in_dim(row_list, place * rows_here, rows_here)
    gate_full, up_full, down_full = (
        lax.all_gather(w_gate, "harm", axis=0, tiled=True),
        lax.all_gather(w_up, "harm", axis=0, tiled=True),
        lax.all_gather(w_down, "harm", axis=0, tiled=True),
    )
    normed = rms_scale(inputs, gain_attn).astype(jnp.bfloat16)
    flat = normed.reshape(length * cols, width)
    qkv = jnp.dot(flat, w_qkv, preferred_element_type=jnp.float32)
    qkv = qkv.astype(jnp.bfloat16).reshape(length, cols, 3 * width)
    a_ell = column_attention(
        split_heads(qkv, 0, split, head_dim),
        split_heads(qkv, width, split, head_dim),
        split_heads(qkv, 2 * width, split, head_dim),
        my_cols,
        scale,
    )
    a_ell = a_ell.reshape(length, cols, split)
    feat_rows = jnp.take(inputs, row_list, axis=0)
    ell_rows = jnp.take(a_ell, row_list, axis=0)
    query_rows = jnp.take(qkv[:, :, split:width], row_list, axis=0)
    key_rows = jnp.take(qkv[:, :, width + split : 2 * width], row_list, axis=0)
    value_rows = jnp.take(qkv[:, :, 2 * width + split :], row_list, axis=0)
    feat_here, ell_here, query_here, key_here, value_here = (
        lax.all_to_all(feat_rows, "harm", split_axis=0, concat_axis=1, tiled=True),
        lax.all_to_all(ell_rows, "harm", split_axis=0, concat_axis=1, tiled=True),
        lax.all_to_all(query_rows, "harm", split_axis=0, concat_axis=1, tiled=True),
        lax.all_to_all(key_rows, "harm", split_axis=0, concat_axis=1, tiled=True),
        lax.all_to_all(value_rows, "harm", split_axis=0, concat_axis=1, tiled=True),
    )
    shape_heads = (rows_here, length, half, head_dim)
    a_m = row_attention(
        query_here.reshape(shape_heads),
        key_here.reshape(shape_heads),
        value_here.reshape(shape_heads),
        col_list,
        my_rows,
        scale,
    )
    attn = jnp.concatenate([ell_here, a_m.reshape(rows_here, length, split)], axis=-1)
    tokens = rows_here * length
    resid = feat_here.astype(jnp.float32).reshape(tokens, width) + jnp.dot(
        attn.reshape(tokens, width), w_out, preferred_element_type=jnp.float32
    )
    normed_ffn = rms_scale(resid, gain_ffn).astype(jnp.bfloat16)
    gate = jnp.dot(normed_ffn, gate_full, preferred_element_type=jnp.float32)
    up = jnp.dot(normed_ffn, up_full, preferred_element_type=jnp.float32)
    hidden = (jax.nn.silu(gate) * up).astype(jnp.bfloat16)
    final = (resid + jnp.dot(hidden, down_full, preferred_element_type=jnp.float32)).reshape(
        rows_here, length, width
    )
    valid = col_list[None, :] <= my_rows[:, None]
    return jnp.where(valid[:, :, None], final, 0.0).astype(jnp.bfloat16)


def solution(mesh):
    placed = (
        P("sample", "harm", None),
        P("sample"),
        P("sample"),
        P(),
        P(),
        P(),
        P(),
        P("harm", None),
        P("harm", None),
        P("harm", None),
    )
    return jax.shard_map(
        per_device, mesh=mesh, in_specs=placed, out_specs=P("harm", "sample", None), check_vma=False
    )
```

profile of v0, /device:TPU:0, one launch (start us, length us, event | category | flops | bytes accessed | tf_op | source)
XLA Modules:
  0.0 141.0 jit_solution(10194991990076802420)
XLA Ops:
  6.5 0.7 all-gather.4.cloned.1.call-update
  7.3 0.7 all-gather.6.cloned.1.call-update
  8.0 0.7 dynamic_slice.7
  8.8 1.2 fusion.15
  10.0 1.2 fusion.17
  14.1 0.7 gather_fusion.1
  16.9 1.1 broadcast_select_fusion.4
  18.0 15.5 %all_to_all.69 = bf16[64,4,256]{2,1,0:T(4,128)(2,1)S(1)} all-to-all(bf16[64,4,256]{2,1,0:T(4,128)(2,1)S(1)} %get-tuple-element.14), channel_id=1, replica_groups=mesh['sample'=2,'harm'=16] {'harm'}, dimensions={0} | all-to-all | bytes 262144 | tf_op jit(solution)/shard_map/all_to_all | solution.py:89
  33.5 3.5 %all-to-all-start.4 = ((bf16[64,4,256]{2,1,0:T(4,128)(2,1)}), bf16[64,4,256]{2,1,0:T(4,128)(2,1)S(1)}, u32[]{:S(2)}, u32[]{:S(2)}) async-start(bf16[64,4,256]{2,1,0:T(4,128)(2,1)} %get-tuple-element.15), calls=%async_computation.4 | async-start | bytes 262144 | tf_op jit(solution)/shard_map/all_to_all | solution.py:90
  37.8 8.1 %all-to-all-done.4 = bf16[64,4,256]{2,1,0:T(4,128)(2,1)S(1)} async-done(((bf16[64,4,256]{2,1,0:T(4,128)(2,1)}), bf16[64,4,256]{2,1,0:T(4,128)(2,1)S(1)}, u32[]{:S(2)}, u32[]{:S(2)}) %all-to-all-start.4) | async-done | bytes 131104 | tf_op jit(solution)/shard_map/all_to_all | solution.py:90
  45.9 3.5 %all-to-all-start.2 = ((bf16[64,4,256]{2,1,0:T(4,128)(2,1)}), bf16[64,4,256]{2,1,0:T(4,128)(2,1)S(1)}, u32[]{:S(2)}, u32[]{:S(2)}) async-start(bf16[64,4,256]{2,1,0:T(4,128)(2,1)} %get-tuple-element.13), calls=%async_computation.2 | async-start | bytes 262144 | tf_op jit(solution)/shard_map/all_to_all | solution.py:91
  49.6 7.7 %all-to-all-done.2 = bf16[64,4,256]{2,1,0:T(4,128)(2,1)S(1)} async-done(((bf16[64,4,256]{2,1,0:T(4,128)(2,1)}), bf16[64,4,256]{2,1,0:T(4,128)(2,1)S(1)}, u32[]{:S(2)}, u32[]{:S(2)}) %all-to-all-start.2) | async-done | bytes 131104 | tf_op jit(solution)/shard_map/all_to_all | solution.py:91
  57.3 3.5 %all-to-all-start.1 = ((bf16[64,4,256]{2,1,0:T(4,128)(2,1)}), bf16[64,4,256]{2,1,0:T(4,128)(2,1)S(1)}, u32[]{:S(2)}, u32[]{:S(2)}) async-start(bf16[64,4,256]{2,1,0:T(4,128)(2,1)} %get-tuple-element.12), calls=%async_computation.1 | async-start | bytes 262144 | tf_op jit(solution)/shard_map/all_to_all | solution.py:88
  60.9 0.8 gather_fusion
  61.7 0.9 broadcast_select_fusion
  63.1 6.5 %all-to-all-done.1 = bf16[64,4,256]{2,1,0:T(4,128)(2,1)S(1)} async-done(((bf16[64,4,256]{2,1,0:T(4,128)(2,1)}), bf16[64,4,256]{2,1,0:T(4,128)(2,1)S(1)}, u32[]{:S(2)}, u32[]{:S(2)}) %all-to-all-start.1) | async-done | bytes 131104 | tf_op jit(solution)/shard_map/all_to_all | solution.py:88
  69.6 3.5 %all-to-all-start = ((bf16[64,4,512]{2,1,0:T(4,128)(2,1)}), bf16[64,4,512]{2,1,0:T(4,128)(2,1)S(1)}, u32[]{:S(2)}, u32[]{:S(2)}) async-start(bf16[64,4,512]{2,1,0:T(4,128)(2,1)} %broadcast_select_fusion), calls=%async_computation | async-start | bytes 524288 | tf_op jit(solution)/shard_map/all_to_all | solution.py:87
  74.6 9.4 %all-to-all-done = bf16[64,4,512]{2,1,0:T(4,128)(2,1)S(1)} async-done(((bf16[64,4,512]{2,1,0:T(4,128)(2,1)}), bf16[64,4,512]{2,1,0:T(4,128)(2,1)S(1)}, u32[]{:S(2)}, u32[]{:S(2)}) %all-to-all-start) | async-done | bytes 262176 | tf_op jit(solution)/shard_map/all_to_all | solution.py:87
  84.3 1.4 %multiply_reduce_fusion = (f32[256]{0:T(256)S(1)}, f32[256,512]{1,0:T(8,128)S(1)}) fusion(f32[256,512]{1,0:T(8,128)S(1)} %reshape.208, bf16[512,512]{1,0:T(8,128)(2,1)} %param.17, bf16[256,256]{1,0:T(8,128)(2,1)S(1)} %concatenate.9, bf16[256,256]{1,0:T(8,128)(2,1)S(1)} %concatenate.8), kind=kOutput, calls=%fused_computation.37 | convolution fusion | flops 135134976 | bytes 1836032 | tf_op jit(solution)/shard_map/dot_general | solution.py:104
  85.7 1.7 %fusion.19 = f32[256,1024]{1,0:T(8,128)S(1)} fusion(bf16[512,1024]{1,0:T(8,128)(2,1)} %all-gather.4.cloned.1.call-done, f32[256,512]{1,0:T(8,128)S(1)} %get-tuple-element.17, f32[512]{0:T(512)S(1)} %copy-done.3, f32[256]{0:T(256)S(1)} %add_rsqrt_fusion.1), kind=kOutput, calls=%fused_computation.40 | convolution fusion | flops 268828672 | bytes 2624512 | tf_op jit(solution)/shard_map/dot_general | solution.py:108
  87.5 4.6 %all-gather.6.cloned.1.call-done = bf16[512,1024]{1,0:T(8,128)(2,1)} async-done(((bf16[32,1024]{1,0:T(8,128)(2,1)}), bf16[512,1024]{1,0:T(8,128)(2,1)}) %all-gather.6.cloned.1.call-update) | async-done | bytes 1048592 | tf_op jit(solution)/shard_map/all_gather | solution.py:66
  92.1 39.1 %all-gather.8.cloned.1.call-done = bf16[1024,512]{1,0:T(8,128)(2,1)} async-done(((bf16[64,512]{1,0:T(8,128)(2,1)}), bf16[1024,512]{1,0:T(8,128)(2,1)}) %all-gather.8.cloned.1.call-update) | async-done | bytes 1048592 | tf_op jit(solution)/shard_map/all_gather | solution.py:67
  131.2 2.4 %convolution_add_fusion = bf16[256,512]{1,0:T(8,128)(2,1)S(1)} fusion(f32[256,512]{1,0:T(8,128)S(1)} %get-tuple-element.17, bf16[1024,512]{1,0:T(8,128)(2,1)} %all-gather.8.cloned.1.call-done, bf16[512,1024]{1,0:T(8,128)(2,1)} %all-gather.6.cloned.1.call-done, f32[256,1024]{1,0:T(8,128)S(1)} %fusion.19, f32[512]{0:T(512)S(1)} %copy-done.3, ...), kind=kOutput, calls=%fused_computation.12 | convolution fusion | flops 539099136 | bytes 3935232 | tf_op jit(solution)/shard_map/dot_general | solution.py:111
  133.6 0.8 select_convert_fusion
  (56 shorter events, 8.3 us)
Async XLA Ops:
  6.5 4.7 %copy-start = (bf16[512,1536]{1,0:T(8,128)(2,1)S(1)}, bf16[512,1536]{1,0:T(8,128)(2,1)}, u32[]{:S(2)}) copy-start(bf16[512,1536]{1,0:T(8,128)(2,1)} %param.16) | copy-start | bytes 4718596
  6.5 79.2 %all-gather.4.cloned.1.call-start = ((), (), s32[]{:S(2)}) async-start(), calls=%async_computation.5 | async-start | bytes 1114112 | tf_op jit(solution)/shard_map/all_gather | solution.py:65
  7.3 84.8 %all-gather.6.cloned.1.call-start = ((), (), s32[]{:S(2)}) async-start(), calls=%async_computation.6 | async-start | bytes 1114112 | tf_op jit(solution)/shard_map/all_gather | solution.py:66
  13.4 0.7 copy-start.4
  14.1 35.3 %copy-start.2 = (s32[64]{0:T(128)S(1)}, s32[64]{0:T(128)}, u32[]{:S(2)}) copy-start(s32[64]{0:T(128)} %param.13) | copy-start | bytes 772
  14.8 46.1 %copy-start.1 = (bf16[64,4,512]{2,1,0:T(4,128)(2,1)S(1)}, bf16[64,4,512]{2,1,0:T(4,128)(2,1)}, u32[]{:S(2)}) copy-start(bf16[64,4,512]{2,1,0:T(4,128)(2,1)} %param.12) | copy-start | bytes 786436
  33.5 12.4 %all-to-all-start.4 = ((bf16[64,4,256]{2,1,0:T(4,128)(2,1)}), bf16[64,4,256]{2,1,0:T(4,128)(2,1)S(1)}, u32[]{:S(2)}, u32[]{:S(2)}) async-start(bf16[64,4,256]{2,1,0:T(4,128)(2,1)} %get-tuple-element.15), calls=%async_computation.4 | async-start | bytes 262144 | tf_op jit(solution)/shard_map/all_to_all | solution.py:90
  37.0 94.2 %all-gather.8.cloned.1.call-start = ((), (), s32[]{:S(2)}) async-start(), calls=%async_computation.7 | async-start | bytes 1114112 | tf_op jit(solution)/shard_map/all_gather | solution.py:67
  45.9 11.4 %all-to-all-start.2 = ((bf16[64,4,256]{2,1,0:T(4,128)(2,1)}), bf16[64,4,256]{2,1,0:T(4,128)(2,1)S(1)}, u32[]{:S(2)}, u32[]{:S(2)}) async-start(bf16[64,4,256]{2,1,0:T(4,128)(2,1)} %get-tuple-element.13), calls=%async_computation.2 | async-start | bytes 262144 | tf_op jit(solution)/shard_map/all_to_all | solution.py:91
  57.3 12.3 %all-to-all-start.1 = ((bf16[64,4,256]{2,1,0:T(4,128)(2,1)}), bf16[64,4,256]{2,1,0:T(4,128)(2,1)S(1)}, u32[]{:S(2)}, u32[]{:S(2)}) async-start(bf16[64,4,256]{2,1,0:T(4,128)(2,1)} %get-tuple-element.12), calls=%async_computation.1 | async-start | bytes 262144 | tf_op jit(solution)/shard_map/all_to_all | solution.py:88
  69.6 14.4 %all-to-all-start = ((bf16[64,4,512]{2,1,0:T(4,128)(2,1)}), bf16[64,4,512]{2,1,0:T(4,128)(2,1)S(1)}, u32[]{:S(2)}, u32[]{:S(2)}) async-start(bf16[64,4,512]{2,1,0:T(4,128)(2,1)} %broadcast_select_fusion), calls=%async_computation | async-start | bytes 524288 | tf_op jit(solution)/shard_map/all_to_all | solution.py:87
  84.1 1.7 %copy-start.3 = (f32[512]{0:T(512)S(1)}, f32[512]{0:T(512)}, u32[]{:S(2)}) copy-start(f32[512]{0:T(512)} %param.18) | copy-start | bytes 6148
Sparse Core Ops, SparseCore 0:
  9.5 42.2 all-gather.3
  54.0 38.0 all-gather.5
  94.2 36.9 all-gather.7
where the time goes:
time: 142 us; the launch traced here: 141 us
  waiting for transfers between devices  77.5 us (55%)
  blocking collectives  15.5 us (11%)
  starting transfers between devices  14.1 us (10%)
  between operations  13.4 us (9%)
  matrix products  7.24 us (5%)
  local copies, waits for them, and re-layouts  7.19 us (5%)
  other arithmetic  5.9 us (4%)
    all_gather x1, waiting for transfers between devices, per_device(): lax.all_gather(w_down, 'harm', axis=0, tiled=True)  39.1 us
    all_to_all x1, blocking collectives, per_device(): lax.all_to_all(query_rows, 'harm', split_axis=0, concat_axis=1, tiled=True)  15.5 us
    all_to_all x1, waiting for transfers between devices, per_device(): lax.all_to_all(feat_rows, 'harm', split_axis=0, concat_axis=1, tiled=True)  9.41 us
    all_to_all x1, waiting for transfers between devices, per_device(): lax.all_to_all(key_rows, 'harm', split_axis=0, concat_axis=1, tiled=True)  8.07 us
    all_to_all x1, waiting for transfers between devices, per_device(): lax.all_to_all(value_rows, 'harm', split_axis=0, concat_axis=1, tiled=True)  7.73 us
    all_to_all x1, waiting for transfers between devices, per_device(): lax.all_to_all(ell_rows, 'harm', split_axis=0, concat_axis=1, tiled=True)  6.48 us
    all_gather x1, waiting for transfers between devices, per_device(): lax.all_gather(w_up, 'harm', axis=0, tiled=True)  4.59 us
    all_to_all x1, starting transfers between devices, per_device(): lax.all_to_all(feat_rows, 'harm', split_axis=0, concat_axis=1, tiled=True)  3.53 us
  transfers between devices with their start and end apart: 7, of which 6 were waited for; matrix products, arithmetic and copies ran while one was open for 12% of the time, Pallas kernels for 0%

commit v1 on v0

--- a/solution.py
+++ b/solution.py
@@ -88,7 +88,12 @@
         lax.all_to_all(ell_rows, "harm", split_axis=0, concat_axis=1, tiled=True),
         lax.all_to_all(query_rows, "harm", split_axis=0, concat_axis=1, tiled=True),
         lax.all_to_all(key_rows, "harm", split_axis=0, concat_axis=1, tiled=True),
-        lax.all_to_all(value_rows, "harm", split_axis=0, concat_axis=1, tiled=True),
+        jnp.concatenate(
+            lax.all_to_all(
+                jnp.stack(jnp.split(value_rows, lax.axis_size("harm"), axis=0)), "harm", 0, 0
+            ),
+            axis=1,
+        ),
     )
     shape_heads = (rows_here, length, half, head_dim)
     a_m = row_attention(

time: 142 us -> 143 us (level)
  blocking collectives: 15.5 us -> 0 us
  starting transfers between devices: 14.1 us -> 24 us
  local copies, waits for them, and re-layouts: 7.19 us -> 16.1 us
  waiting for transfers between devices: 77.5 us -> 75.4 us
    all_to_all x1 -> x0, blocking collectives: 15.5 us -> none  [per_device(): lax.all_to_all(query_rows, 'harm', split_axis=0, concat_axis=1, tiled=True)]
    unnamed x10 -> x25, local copies, waits for them, and re-layouts: 0.24 us -> 9.22 us
    all_to_all x1 -> x2, starting transfers between devices: 3.51 us -> 10.9 us  [the longest x1 7.36 us: per_device(): lax.all_to_all(query_rows, 'harm', split_axis=0, concat_axis=1, tiled=True)]
    all_gather x1, waiting for transfers between devices: 4.59 us -> 1.33 us  [per_device(): lax.all_gather(w_up, 'harm', axis=0, tiled=True)]
    all_to_all x1, starting transfers between devices: 3.51 us -> 6.01 us  [per_device(): lax.all_to_all(key_rows, 'harm', split_axis=0, concat_axis=1, tiled=True)]
    all_to_all x1, waiting for transfers between devices: 9.41 us -> 11 us  [per_device(): lax.all_to_all(feat_rows, 'harm', split_axis=0, concat_axis=1, tiled=True)]
    all_to_all x1 -> x2, waiting for transfers between devices: 7.73 us -> 7.78 us  [the longest x1 7.78 us: per_device(): lax.all_to_all(jnp.stack(jnp.split(value_rows, lax.axis_size('harm'), axi...]
  transfers between devices with their start and end apart: 7 -> 8, of which waited for: 6 -> 6; matrix products, arithmetic and copies ran while one was open for 12% -> 18% of each run, Pallas kernels for 0% -> 0%
where the time goes in v1:
time: 143 us; the launch traced here: 142 us
  waiting for transfers between devices  75.4 us (53%)
  starting transfers between devices  24 us (17%)
  local copies, waits for them, and re-layouts  16.1 us (11%)
  between operations  13.5 us (9%)
  matrix products  7.15 us (5%)
  other arithmetic  5.89 us (4%)
    all_gather x1, waiting for transfers between devices, per_device(): lax.all_gather(w_down, 'harm', axis=0, tiled=True)  40.1 us
    all_to_all x1, waiting for transfers between devices, per_device(): lax.all_to_all(feat_rows, 'harm', split_axis=0, concat_axis=1, tiled=True)  11 us
    unnamed x25, local copies, waits for them, and re-layouts  9.22 us
    all_to_all x1, waiting for transfers between devices, per_device(): lax.all_to_all(jnp.stack(jnp.split(value_rows, lax.axis_size('harm'), axi...  7.78 us
    all_to_all x1, waiting for transfers between devices, per_device(): lax.all_to_all(key_rows, 'harm', split_axis=0, concat_axis=1, tiled=True)  7.37 us
    all_to_all x1, starting transfers between devices, per_device(): lax.all_to_all(query_rows, 'harm', split_axis=0, concat_axis=1, tiled=True)  7.36 us
    all_to_all x1, starting transfers between devices, per_device(): lax.all_to_all(key_rows, 'harm', split_axis=0, concat_axis=1, tiled=True)  6.01 us
    all_to_all x1, waiting for transfers between devices, per_device(): lax.all_to_all(ell_rows, 'harm', split_axis=0, concat_axis=1, tiled=True)  5.72 us
  transfers between devices with their start and end apart: 8, of which 6 were waited for; matrix products, arithmetic and copies ran while one was open for 18% of the time, Pallas kernels for 0%

profile of v1, /device:TPU:0, one launch (start us, length us, event | category | flops | bytes accessed | tf_op | source)
XLA Modules:
  0.0 142.0 jit_solution(8976134450344202523)
XLA Ops:
  6.5 0.7 all-gather.4.cloned.1.call-update
  7.3 0.7 all-gather.6.cloned.1.call-update
  8.0 1.2 fusion.15
  9.2 1.2 fusion.17
  14.1 0.7 gather_fusion.2
  14.9 0.7 gather_fusion.3
  16.3 1.1 broadcast_select_fusion.4
  17.3 7.4 %all-to-all-start.3 = ((bf16[64,4,256]{2,1,0:T(4,128)(2,1)}), bf16[64,4,256]{2,1,0:T(4,128)(2,1)S(1)}, u32[]{:S(2)}, u32[]{:S(2)}) async-start(bf16[64,4,256]{2,1,0:T(4,128)(2,1)} %get-tuple-element.14), calls=%async_computation.3 | async-start | bytes 262144 | tf_op jit(solution)/shard_map/all_to_all | solution.py:89
  33.8 6.0 %all-to-all-start.4 = ((bf16[64,4,256]{2,1,0:T(4,128)(2,1)}), bf16[64,4,256]{2,1,0:T(4,128)(2,1)S(1)}, u32[]{:S(2)}, u32[]{:S(2)}) async-start(bf16[64,4,256]{2,1,0:T(4,128)(2,1)} %get-tuple-element.15), calls=%async_computation.4 | async-start | bytes 262144 | tf_op jit(solution)/shard_map/all_to_all | solution.py:90
  41.1 7.4 %all-to-all-done.4 = bf16[64,4,256]{2,1,0:T(4,128)(2,1)S(1)} async-done(((bf16[64,4,256]{2,1,0:T(4,128)(2,1)}), bf16[64,4,256]{2,1,0:T(4,128)(2,1)S(1)}, u32[]{:S(2)}, u32[]{:S(2)}) %all-to-all-start.4) | async-done | bytes 131104 | tf_op jit(solution)/shard_map/all_to_all | solution.py:90
  48.5 3.5 %all-to-all-start.2 = ((bf16[16,4,4,256]{3,2,1,0:T(4,128)(2,1)}), bf16[16,4,4,256]{3,2,1,0:T(4,128)(2,1)S(1)}, u32[]{:S(2)}, u32[]{:S(2)}) async-start(bf16[16,4,4,256]{3,2,1,0:T(4,128)(2,1)} %constant_dynamic-update-slice_fusion), calls=%async_computation.2 | async-start | bytes 262144 | tf_op jit(solution)/shard_map/all_to_all | solution.py:92
  52.2 7.8 %all-to-all-done.2 = bf16[16,4,4,256]{3,2,1,0:T(4,128)(2,1)S(1)} async-done(((bf16[16,4,4,256]{3,2,1,0:T(4,128)(2,1)}), bf16[16,4,4,256]{3,2,1,0:T(4,128)(2,1)S(1)}, u32[]{:S(2)}, u32[]{:S(2)}) %all-to-all-start.2) | async-done | bytes 131104 | tf_op jit(solution)/shard_map/all_to_all | solution.py:92
  59.9 3.5 %all-to-all-start.1 = ((bf16[64,4,256]{2,1,0:T(4,128)(2,1)}), bf16[64,4,256]{2,1,0:T(4,128)(2,1)S(1)}, u32[]{:S(2)}, u32[]{:S(2)}) async-start(bf16[64,4,256]{2,1,0:T(4,128)(2,1)} %get-tuple-element.12), calls=%async_computation.1 | async-start | bytes 262144 | tf_op jit(solution)/shard_map/all_to_all | solution.py:88
  63.6 0.8 gather_fusion
  64.4 0.9 broadcast_select_fusion
  65.8 5.7 %all-to-all-done.1 = bf16[64,4,256]{2,1,0:T(4,128)(2,1)S(1)} async-done(((bf16[64,4,256]{2,1,0:T(4,128)(2,1)}), bf16[64,4,256]{2,1,0:T(4,128)(2,1)S(1)}, u32[]{:S(2)}, u32[]{:S(2)}) %all-to-all-start.1) | async-done | bytes 131104 | tf_op jit(solution)/shard_map/all_to_all | solution.py:88
  71.5 3.5 %all-to-all-start = ((bf16[64,4,512]{2,1,0:T(4,128)(2,1)}), bf16[64,4,512]{2,1,0:T(4,128)(2,1)S(1)}, u32[]{:S(2)}, u32[]{:S(2)}) async-start(bf16[64,4,512]{2,1,0:T(4,128)(2,1)} %broadcast_select_fusion), calls=%async_computation | async-start | bytes 524288 | tf_op jit(solution)/shard_map/all_to_all | solution.py:87
  76.5 11.0 %all-to-all-done = bf16[64,4,512]{2,1,0:T(4,128)(2,1)S(1)} async-done(((bf16[64,4,512]{2,1,0:T(4,128)(2,1)}), bf16[64,4,512]{2,1,0:T(4,128)(2,1)S(1)}, u32[]{:S(2)}, u32[]{:S(2)}) %all-to-all-start) | async-done | bytes 262176 | tf_op jit(solution)/shard_map/all_to_all | solution.py:87
  87.7 1.4 %multiply_reduce_fusion = (f32[256]{0:T(256)S(1)}, f32[256,512]{1,0:T(8,128)S(1)}) fusion(f32[256,512]{1,0:T(8,128)S(1)} %reshape.207, bf16[512,512]{1,0:T(8,128)(2,1)} %param.17, bf16[256,256]{1,0:T(8,128)(2,1)S(1)} %concatenate.9, bf16[256,256]{1,0:T(8,128)(2,1)S(1)} %concatenate.8), kind=kOutput, calls=%fused_computation.37 | convolution fusion | flops 135134976 | bytes 1836032 | tf_op jit(solution)/shard_map/dot_general | solution.py:109
  89.2 1.7 %fusion.19 = f32[256,1024]{1,0:T(8,128)S(1)} fusion(bf16[512,1024]{1,0:T(8,128)(2,1)} %all-gather.4.cloned.1.call-done, f32[256,512]{1,0:T(8,128)S(1)} %get-tuple-element.17, f32[512]{0:T(512)S(1)} %copy-done.3, f32[256]{0:T(256)S(1)} %add_rsqrt_fusion.1), kind=kOutput, calls=%fused_computation.40 | convolution fusion | flops 268828672 | bytes 2624512 | tf_op jit(solution)/shard_map/dot_general | solution.py:113
  90.9 1.3 all-gather.6.cloned.1.call-done
  92.2 40.1 %all-gather.8.cloned.1.call-done = bf16[1024,512]{1,0:T(8,128)(2,1)} async-done(((bf16[64,512]{1,0:T(8,128)(2,1)}), bf16[1024,512]{1,0:T(8,128)(2,1)}) %all-gather.8.cloned.1.call-update) | async-done | bytes 1048592 | tf_op jit(solution)/shard_map/all_gather | solution.py:67
  132.3 2.3 %convolution_add_fusion = bf16[256,512]{1,0:T(8,128)(2,1)S(1)} fusion(f32[256,512]{1,0:T(8,128)S(1)} %get-tuple-element.17, bf16[1024,512]{1,0:T(8,128)(2,1)} %all-gather.8.cloned.1.call-done, bf16[512,1024]{1,0:T(8,128)(2,1)} %all-gather.6.cloned.1.call-done, f32[256,1024]{1,0:T(8,128)S(1)} %fusion.19, f32[512]{0:T(512)S(1)} %copy-done.3, ...), kind=kOutput, calls=%fused_computation.12 | convolution fusion | flops 539099136 | bytes 3935232 | tf_op jit(solution)/shard_map/dot_general | solution.py:116
  134.7 0.8 select_convert_fusion
  (73 shorter events, 17.2 us)
Async XLA Ops:
  6.5 3.9 %copy-start = (bf16[512,1536]{1,0:T(8,128)(2,1)S(1)}, bf16[512,1536]{1,0:T(8,128)(2,1)}, u32[]{:S(2)}) copy-start(bf16[512,1536]{1,0:T(8,128)(2,1)} %param.16) | copy-start | bytes 4718596
  6.5 82.6 %all-gather.4.cloned.1.call-start = ((), (), s32[]{:S(2)}) async-start(), calls=%async_computation.5 | async-start | bytes 1114112 | tf_op jit(solution)/shard_map/all_gather | solution.py:65
  7.3 85.0 %all-gather.6.cloned.1.call-start = ((), (), s32[]{:S(2)}) async-start(), calls=%async_computation.6 | async-start | bytes 1114112 | tf_op jit(solution)/shard_map/all_gather | solution.py:66
  11.2 0.9 copy-start.2
  12.8 0.7 copy-start.4
  14.8 48.7 %copy-start.1 = (bf16[64,4,512]{2,1,0:T(4,128)(2,1)S(1)}, bf16[64,4,512]{2,1,0:T(4,128)(2,1)}, u32[]{:S(2)}) copy-start(bf16[64,4,512]{2,1,0:T(4,128)(2,1)} %param.12) | copy-start | bytes 786436
  17.3 16.5 %all-to-all-start.3 = ((bf16[64,4,256]{2,1,0:T(4,128)(2,1)}), bf16[64,4,256]{2,1,0:T(4,128)(2,1)S(1)}, u32[]{:S(2)}, u32[]{:S(2)}) async-start(bf16[64,4,256]{2,1,0:T(4,128)(2,1)} %get-tuple-element.14), calls=%async_computation.3 | async-start | bytes 262144 | tf_op jit(solution)/shard_map/all_to_all | solution.py:89
  24.7 107.7 %all-gather.8.cloned.1.call-start = ((), (), s32[]{:S(2)}) async-start(), calls=%async_computation.7 | async-start | bytes 1114112 | tf_op jit(solution)/shard_map/all_gather | solution.py:67
  33.8 14.7 %all-to-all-start.4 = ((bf16[64,4,256]{2,1,0:T(4,128)(2,1)}), bf16[64,4,256]{2,1,0:T(4,128)(2,1)S(1)}, u32[]{:S(2)}, u32[]{:S(2)}) async-start(bf16[64,4,256]{2,1,0:T(4,128)(2,1)} %get-tuple-element.15), calls=%async_computation.4 | async-start | bytes 262144 | tf_op jit(solution)/shard_map/all_to_all | solution.py:90
  48.5 11.5 %all-to-all-start.2 = ((bf16[16,4,4,256]{3,2,1,0:T(4,128)(2,1)}), bf16[16,4,4,256]{3,2,1,0:T(4,128)(2,1)S(1)}, u32[]{:S(2)}, u32[]{:S(2)}) async-start(bf16[16,4,4,256]{3,2,1,0:T(4,128)(2,1)} %constant_dynamic-update-slice_fusion), calls=%async_computation.2 | async-start | bytes 262144 | tf_op jit(solution)/shard_map/all_to_all | solution.py:92
  59.9 11.5 %all-to-all-start.1 = ((bf16[64,4,256]{2,1,0:T(4,128)(2,1)}), bf16[64,4,256]{2,1,0:T(4,128)(2,1)S(1)}, u32[]{:S(2)}, u32[]{:S(2)}) async-start(bf16[64,4,256]{2,1,0:T(4,128)(2,1)} %get-tuple-element.12), calls=%async_computation.1 | async-start | bytes 262144 | tf_op jit(solution)/shard_map/all_to_all | solution.py:88
  71.5 16.0 %all-to-all-start = ((bf16[64,4,512]{2,1,0:T(4,128)(2,1)}), bf16[64,4,512]{2,1,0:T(4,128)(2,1)S(1)}, u32[]{:S(2)}, u32[]{:S(2)}) async-start(bf16[64,4,512]{2,1,0:T(4,128)(2,1)} %broadcast_select_fusion), calls=%async_computation | async-start | bytes 524288 | tf_op jit(solution)/shard_map/all_to_all | solution.py:87
  87.5 1.7 %copy-start.3 = (f32[512]{0:T(512)S(1)}, f32[512]{0:T(512)}, u32[]{:S(2)}) copy-start(f32[512]{0:T(512)} %param.18) | copy-start | bytes 6148
Sparse Core Ops, SparseCore 0:
  9.5 41.0 all-gather.3
  52.8 39.3 all-gather.5
  94.4 37.8 all-gather.7
